TPU v7x, 32 devices: a whole 2x2x4 slice. The times are simulated.
32 devices in a mesh: tm: 2 (over core), lat: 16 (over z, y, x).
Axes of the slice: x: 2, y: 2, z: 4, core: 2. Of those that a mesh axis runs over, the one named last changes fastest.
Arguments:
- spectral_state: float32 [4, 16, 2, 16, 256], P('tm', 'lat'), may hold values from -6 to 6
- legendre: bfloat16 [16, 16, 16], P('lat'), may hold values from -1.5 to 1.5
- wave_slots: int32 [16], replicated, may hold values from 0 to 15, each once
- lat_order: int32 [16], replicated, may hold values from 0 to 15, each once
- quad_weights: float32 [16], replicated, may hold values from 0.2 to 1
- available: int32 [4, 8, 16, 256], P('tm', None, 'lat'), may hold values 0 or 1
- targets: float32 [4, 4, 8], P('tm'), may hold values from -6 to 6
- w_first: float32 [256, 384], replicated, may hold values from -0.375 to 0.375
- w_mid: float32 [384, 384], replicated, may hold values from -0.3125 to 0.3125
- w_last: float32 [384, 256], replicated, may hold values from -0.3125 to 0.3125
- norm_bias: float32 [2, 1024], replicated, may hold values from -0.3 to 0.3
- mean_first: float32 [256, 384], replicated, may hold values from -0.00061035156 to 0.00061035156
- mean_mid: float32 [384, 384], replicated, may hold values from -0.00061035156 to 0.00061035156
- mean_last: float32 [384, 256], replicated, may hold values from -0.00061035156 to 0.00061035156
- mean_bias: float32 [2, 1024], replicated, may hold values from -0.00061035156 to 0.00061035156
- square_first: float32 [256, 384], replicated, may hold values from 3e-10 to 3e-08
- square_mid: float32 [384, 384], replicated, may hold values from 3e-10 to 3e-08
- square_last: float32 [384, 256], replicated, may hold values from 3e-10 to 3e-08
- square_bias: float32 [2, 1024], replicated, may hold values from 3e-10 to 3e-08
Outputs:
- loss: float32 [], replicated
- grad_norm: float32 [], replicated
- master_first: float32 [256, 384], replicated
- master_mid: float32 [384, 384], replicated
- master_last: float32 [384, 256], replicated
- master_bias: float32 [2, 1024], replicated
- new_mean_first: float32 [256, 384], replicated
- new_mean_mid: float32 [384, 384], replicated
- new_mean_last: float32 [384, 256], replicated
- new_mean_bias: float32 [2, 1024], replicated
- new_square_first: float32 [256, 384], replicated
- new_square_mid: float32 [384, 384], replicated
- new_square_last: float32 [384, 256], replicated
- new_square_bias: float32 [2, 1024], replicated
- half_first: bfloat16 [256, 384], replicated
- half_mid: bfloat16 [384, 384], replicated
- half_last: bfloat16 [384, 256], replicated
- half_bias: bfloat16 [2, 1024], replicated
Inputs may be any that keep to these rules, and one draw needn't show every extreme that they name: `wave_slots`: each wavenumber 0 to 15 stands in one slot; slot j lies on the device of index j // 1 of lat. `lat_order`: each latitude stands in one grid row.
All inputs are finite; a program needn't handle non-finite values. No bound on the sum of `available` on one device may be relied on, other than what follows from the above.
Results may differ from a plain program's by a relative error of at most 0.0082.
Values may be sent and summed in bfloat16 or wider, within the bound.
No kernel may reach another device: no remote copies, remote signals or barrier semaphores. Data moves between devices by JAX's collectives and lax.ppermute only.
A program may use at most 128 MiB of HBM per device.

v0:
```python
from functools import partial
import math
import jax
import jax.numpy as jnp
from jax import lax
from jax.sharding import PartitionSpec as P

STEPS = 4
EPS_NORM = 1e-05
STEP_SCALE = 0.5
CLIP_NORM = 1.0
LEARN_RATE = 0.01
BETA_ONE = 0.9
BETA_TWO = 0.95
EPS_ADAM = 1e-08
DECAY = 0.1
HIGH = lax.Precision.HIGHEST


def wave_tables(wave_slots, lon_count):
    product = wave_slots[:, None] * jnp.arange(lon_count, dtype=jnp.int32)[None, :] % lon_count
    phase = product.astype(jnp.float32) * (2.0 * math.pi / lon_count)
    inverse = jnp.stack([jnp.cos(phase), -jnp.sin(phase)], axis=1)
    scale = jnp.where(wave_slots == 0, 1.0, 2.0).astype(jnp.float32) / lon_count
    return (inverse.astype(jnp.bfloat16), (inverse * scale[:, None, None]).astype(jnp.bfloat16))


def layer_spans(chans, hidden):
    gains = [(0, chans), (chans, hidden), (chans + hidden, hidden)]
    biases = [(0, hidden), (hidden, hidden), (2 * hidden, chans)]
    return list(zip(gains, biases))


def norm_gain(x, gain):
    centre = x - jnp.mean(x, axis=-1, keepdims=True)
    return centre * lax.rsqrt(jnp.mean(centre * centre, axis=-1, keepdims=True) + EPS_NORM) * gain


def corrector_forward(x, weights, norm_bias):
    spans = layer_spans(weights[0].shape[0], weights[0].shape[1])
    saved = []
    for k in range(3):
        (gstart, gwidth), (bstart, bwidth) = spans[k]
        h_low = norm_gain(x, 1.0 + norm_bias[0, gstart : gstart + gwidth]).astype(jnp.bfloat16)
        z_val = (
            jnp.dot(h_low, weights[k], preferred_element_type=jnp.float32)
            + norm_bias[1, bstart : bstart + bwidth]
        )
        saved.append((x, h_low, z_val))
        x = jax.nn.gelu(z_val, approximate=False) if k < 2 else z_val
    return (x, saved)


def corrector_backward(grad, saved, weights, norm_bias):
    spans = layer_spans(weights[0].shape[0], weights[0].shape[1])
    weight_grads = [None, None, None]
    gain_parts = [None, None, None]
    bias_parts = [None, None, None]
    for k in (2, 1, 0):
        (gstart, gwidth), (bstart, bwidth) = spans[k]
        x, h_low, z_val = saved[k]
        if k < 2:
            grad = jax.vjp(partial(jax.nn.gelu, approximate=False), z_val)[1](grad)[0]
        grad_low = grad.astype(jnp.bfloat16)
        weight_grads[k] = lax.dot_general(
            h_low, grad_low, (((0,), (0,)), ((), ())), preferred_element_type=jnp.float32
        )
        bias_parts[k] = jnp.sum(grad_low, axis=0, dtype=jnp.float32)
        back_h = lax.dot_general(
            grad_low, weights[k], (((1,), (1,)), ((), ())), preferred_element_type=jnp.float32
        )
        grad, gain_parts[k] = jax.vjp(norm_gain, x, 1.0 + norm_bias[0, gstart : gstart + gwidth])[
            1
        ](back_h)
    vector_grad = jnp.stack([jnp.concatenate(gain_parts), jnp.concatenate(bias_parts)])
    return (grad, (weight_grads[0], weight_grads[1], weight_grads[2], vector_grad))


def adamw(weight, mean, square, grad):
    mean_new = BETA_ONE * mean + (1.0 - BETA_ONE) * grad
    square_new = BETA_TWO * square + (1.0 - BETA_TWO) * grad * grad
    weight_new = weight - LEARN_RATE * (
        mean_new / (jnp.sqrt(square_new) + EPS_ADAM) + DECAY * weight
    )
    return (weight_new, mean_new, square_new)


def per_device(
    spectral_state,
    legendre,
    wave_slots,
    lat_order,
    quad_weights,
    available,
    targets,
    w_first,
    w_mid,
    w_last,
    norm_bias,
    mean_first,
    mean_mid,
    mean_last,
    mean_bias,
    square_first,
    square_mid,
    square_last,
    square_bias,
):
    tdev, wdev, _, degrees, chans = spectral_state.shape
    fields = available.shape[1]
    rows_dev = available.shape[2]
    lon_count = available.shape[3]
    levels = chans // fields
    lat_index = lax.axis_index("lat")
    slots = lax.dynamic_slice_in_dim(wave_slots, lat_index * wdev, wdev)
    finv, ffw = wave_tables(wave_slots, lon_count)
    keep = (jnp.arange(degrees, dtype=jnp.int32)[None, :] >= slots[:, None]).astype(jnp.bfloat16)
    plg = jnp.take(legendre, lat_order, axis=2) * keep[:, :, None]
    qrow = jnp.take(quad_weights, lat_order)
    qlocal = lax.dynamic_slice_in_dim(qrow, lat_index * rows_dev, rows_dev)
    colw = qlocal[None, None, :, None] * available.astype(jnp.float32)
    den_part = jnp.sum(colw, axis=(2, 3))
    params = (w_first, w_mid, w_last, norm_bias)
    weights = (
        w_first.astype(jnp.bfloat16),
        w_mid.astype(jnp.bfloat16),
        w_last.astype(jnp.bfloat16),
    )

    def legendre_sum(piece):
        return jnp.einsum("mnr,tmprc->tmpnc", plg, piece, preferred_element_type=jnp.float32)

    def fourier_sum(table, piece):
        return jnp.einsum("mpk,tmprc->trkc", table, piece, preferred_element_type=jnp.float32)

    def to_grid(state):
        sums = jnp.einsum(
            "mnr,tmpnc->tmprc", plg, state.astype(jnp.bfloat16), preferred_element_type=jnp.float32
        ).astype(jnp.bfloat16)
        return fourier_sum(
            finv, lax.all_to_all(sums, "lat", split_axis=3, concat_axis=1, tiled=True)
        )

    def column_pass(grid):
        out, saved = corrector_forward(grid.reshape(-1, chans), weights, norm_bias)
        return (out.reshape(grid.shape), saved)

    states = []
    nums = []
    den_total = den_part
    state = spectral_state
    for s in range(STEPS):
        states.append(state)
        grid = to_grid(state)
        out, saved = column_pass(grid)
        pred = grid + STEP_SCALE * out
        num_part = jnp.einsum(
            "tfrk,trkfl->tf",
            colw,
            pred.reshape(tdev, rows_dev, lon_count, fields, levels),
            precision=HIGH,
        )
        num_total, den_total = lax.psum((num_part, den_part), "lat")
        nums.append(num_total)
        tend = (out * qlocal[None, :, None, None]).astype(jnp.bfloat16)
        coeff = jnp.einsum("mpk,trkc->tmprc", ffw, tend, preferred_element_type=jnp.float32).astype(
            jnp.bfloat16
        )
        spec = legendre_sum(lax.all_to_all(coeff, "lat", split_axis=1, concat_axis=3, tiled=True))
        state = state + STEP_SCALE * spec
    num_all = jnp.stack(nums)
    bias = num_all / (levels * den_total[None]) - jnp.moveaxis(targets, 1, 0)
    loss = lax.psum(jnp.sum(bias * bias) / STEPS, "tm")
    grad_bias = 2.0 * bias / (STEPS * levels * den_total[None])
    totals = tuple((jnp.zeros_like(p) for p in params))
    back_state = None
    for s in reversed(range(STEPS)):
        grid = to_grid(states[s])
        out, saved = column_pass(grid)
        scaled = jnp.moveaxis(colw * grad_bias[s][:, :, None, None], 1, 3)
        back_pred = jnp.broadcast_to(scaled[..., None], scaled.shape + (levels,)).reshape(
            grid.shape
        )
        back_out = STEP_SCALE * back_pred
        if back_state is not None:
            back_spec = (STEP_SCALE * back_state).astype(jnp.bfloat16)
            back_coeff = jnp.einsum(
                "mnr,tmpnc->tmprc", plg, back_spec, preferred_element_type=jnp.float32
            ).astype(jnp.bfloat16)
            back_tend = fourier_sum(
                ffw, lax.all_to_all(back_coeff, "lat", split_axis=3, concat_axis=1, tiled=True)
            )
            back_out = back_out + qlocal[None, :, None, None] * back_tend
        back_in, grads = corrector_backward(back_out.reshape(-1, chans), saved, weights, norm_bias)
        totals = tuple((a + b for a, b in zip(totals, grads)))
        if s > 0:
            back_grid = (back_pred + back_in.reshape(grid.shape)).astype(jnp.bfloat16)
            back_sums = jnp.einsum(
                "mpk,trkc->tmprc", finv, back_grid, preferred_element_type=jnp.float32
            ).astype(jnp.bfloat16)
            back_low = legendre_sum(
                lax.all_to_all(back_sums, "lat", split_axis=1, concat_axis=3, tiled=True)
            )
            back_state = back_low if back_state is None else back_state + back_low
    means = (mean_first, mean_mid, mean_last, mean_bias)
    squares = (square_first, square_mid, square_last, square_bias)
    grads = lax.psum(totals, ("tm", "lat"))
    grad_norm = jnp.sqrt(sum((jnp.sum(g * g) for g in grads)))
    factor = CLIP_NORM / jnp.maximum(grad_norm, CLIP_NORM)
    results = [adamw(w, a, b, g * factor) for w, a, b, g in zip(params, means, squares, grads)]
    masters = [r[0] for r in results]
    new_means = [r[1] for r in results]
    new_squares = [r[2] for r in results]
    halves = [w.astype(jnp.bfloat16) for w in masters]
    return (
        loss,
        grad_norm,
        masters[0],
        masters[1],
        masters[2],
        masters[3],
        new_means[0],
        new_means[1],
        new_means[2],
        new_means[3],
        new_squares[0],
        new_squares[1],
        new_squares[2],
        new_squares[3],
        halves[0],
        halves[1],
        halves[2],
        halves[3],
    )


def solution(mesh):
    in_specs = (
        P("tm", "lat", None, None, None),
        P("lat", None, None),
        P(),
        P(),
        P(),
        P("tm", None, "lat", None),
        P("tm", None, None),
        P(),
        P(),
        P(),
        P(),
        P(),
        P(),
        P(),
        P(),
        P(),
        P(),
        P(),
        P(),
    )
    out_specs = (
        P(),
        P(),
        P(),
        P(),
        P(),
        P(),
        P(),
        P(),
        P(),
        P(),
        P(),
        P(),
        P(),
        P(),
        P(),
        P(),
        P(),
        P(),
    )
    return jax.shard_map(
        per_device, mesh=mesh, in_specs=in_specs, out_specs=out_specs, check_vma=False
    )
```

profile of v0, /device:TPU:0, one launch (start us, length us, event | category | flops | bytes accessed | tf_op | source)
XLA Modules:
  0.0 490.8 jit_solution(849199737556524078)
XLA Ops:
  11.4 8.3 %all-to-all-start = ((bf16[2,1,2,16,256]{4,2,0,1,3:T(2,128)(2,1)}), bf16[2,1,2,16,256]{4,2,0,1,3:T(2,128)(2,1)S(1)}, u32[]{:S(2)}, u32[]{:S(2)}) async-start(bf16[2,1,2,16,256]{4,2,0,1,3:T(2,128)(2,1)} %copy.194), calls=%async_computation | async-start | bytes 65536 | tf_op jit(solution)/shard_map/all_to_all | solution.py:141
  21.9 5.3 %all-to-all-done = bf16[2,1,2,16,256]{4,2,0,1,3:T(2,128)(2,1)S(1)} async-done(((bf16[2,1,2,16,256]{4,2,0,1,3:T(2,128)(2,1)}), bf16[2,1,2,16,256]{4,2,0,1,3:T(2,128)(2,1)S(1)}, u32[]{:S(2)}, u32[]{:S(2)}) %all-to-all-start) | async-done | bytes 32800 | tf_op jit(solution)/shard_map/all_to_all | solution.py:141
  28.0 3.0 fusion.214
  31.9 3.2 fusion.212
  37.8 10.0 %all_to_all.215 = bf16[2,16,2,1,256]{4,2,0,3,1:T(2,128)(2,1)S(1)} all-to-all(bf16[2,16,2,1,256]{4,2,0,3,1:T(2,128)(2,1)S(1)} %copy.198), channel_id=1, replica_groups=mesh['tm'=2,'lat'=16] {'lat'}, dimensions={1} | all-to-all | bytes 65536 | tf_op jit(solution)/shard_map/all_to_all | solution.py:169
  48.2 10.1 %all_to_all.216 = bf16[2,1,2,16,256]{4,2,0,1,3:T(2,128)(2,1)S(1)} all-to-all(bf16[2,1,2,16,256]{4,2,0,1,3:T(2,128)(2,1)S(1)} %copy.202), channel_id=1, replica_groups=mesh['tm'=2,'lat'=16] {'lat'}, dimensions={3} | all-to-all | bytes 65536 | tf_op jit(solution)/shard_map/all_to_all | solution.py:141
  60.6 3.0 fusion.210
  64.5 3.2 fusion.208
  70.5 10.0 %all_to_all.217 = bf16[2,16,2,1,256]{4,2,0,3,1:T(2,128)(2,1)S(1)} all-to-all(bf16[2,16,2,1,256]{4,2,0,3,1:T(2,128)(2,1)S(1)} %copy.206), channel_id=1, replica_groups=mesh['tm'=2,'lat'=16] {'lat'}, dimensions={1} | all-to-all | bytes 65536 | tf_op jit(solution)/shard_map/all_to_all | solution.py:169
  80.8 10.0 %all_to_all.218 = bf16[2,1,2,16,256]{4,2,0,1,3:T(2,128)(2,1)S(1)} all-to-all(bf16[2,1,2,16,256]{4,2,0,1,3:T(2,128)(2,1)S(1)} %copy.209), channel_id=1, replica_groups=mesh['tm'=2,'lat'=16] {'lat'}, dimensions={3} | all-to-all | bytes 65536 | tf_op jit(solution)/shard_map/all_to_all | solution.py:141
  93.4 3.1 fusion.206
  96.7 3.2 fusion.204
  100.0 1.9 broadcast_multiply_fusion
  102.1 10.0 %all_to_all.219 = bf16[2,16,2,1,256]{4,2,0,3,1:T(2,128)(2,1)S(1)} all-to-all(bf16[2,16,2,1,256]{4,2,0,3,1:T(2,128)(2,1)S(1)} %copy.213), channel_id=1, replica_groups=mesh['tm'=2,'lat'=16] {'lat'}, dimensions={1} | all-to-all | bytes 65536 | tf_op jit(solution)/shard_map/all_to_all | solution.py:169
  113.0 3.8 all-to-all-start.6
  117.7 2.0 copy.197
  122.8 2.1 copy.205
  124.9 1.9 add.549
  127.9 2.1 copy.212
  130.0 1.9 add.558
  136.3 3.1 fusion.202
  140.6 3.2 fusion.200
  145.1 2.1 copy.219
  147.2 2.1 add.567
  150.4 42.5 %all-reduce.1 = (f32[1,2,8]{2,1,0:T(2,128)S(1)}, f32[1,2,8]{2,1,0:T(2,128)S(1)}, f32[1,2,8]{2,1,0:T(2,128)S(1)}, f32[1,2,8]{2,1,0:T(2,128)S(1)}, f32[2,8]{1,0:T(2,128)S(1)}) all-reduce(f32[1,2,8]{2,1,0:T(2,128)S(1)} %bitcast.673, f32[1,2,8]{2,1,0:T(2,128)S(1)} %bitcast.674, ...), channel_id=1, replica_groups=mesh['tm'=2,'lat'=16] {'lat'}, use_global_device_ids=true, to_apply=%region_31.32 | all-reduce | flops 80 | bytes 640 | tf_op jit(solution)/shard_map/psum | solution.py:163
  203.2 1.9 convert_reduce_fusion.7
  205.1 2.8 multiply_reduce_fusion.27
  208.6 2.2 fusion.220
  210.8 3.4 psum.75
  218.5 2.0 copy.233
  221.4 2.0 copy.253
  224.2 2.0 copy.243
  230.8 3.6 all-to-all-start.7
  235.2 6.7 %all-to-all-done.7 = bf16[2,16,2,1,256]{4,2,0,3,1:T(2,128)(2,1)S(1)} async-done(((bf16[2,16,2,1,256]{4,2,0,3,1:T(2,128)(2,1)}), bf16[2,16,2,1,256]{4,2,0,3,1:T(2,128)(2,1)S(1)}, u32[]{:S(2)}, u32[]{:S(2)}) %all-to-all-start.7) | async-done | bytes 32800 | tf_op jit(solution)/shard_map/all_to_all | solution.py:202
  242.8 3.5 all-to-all-start.8
  247.0 6.6 %all-to-all-done.8 = bf16[2,1,2,16,256]{4,2,0,1,3:T(2,128)(2,1)S(1)} async-done(((bf16[2,1,2,16,256]{4,2,0,1,3:T(2,128)(2,1)}), bf16[2,1,2,16,256]{4,2,0,1,3:T(2,128)(2,1)S(1)}, u32[]{:S(2)}, u32[]{:S(2)}) %all-to-all-start.8) | async-done | bytes 32800 | tf_op jit(solution)/shard_map/all_to_all | solution.py:191
  253.7 2.0 convert_reduce_fusion.10
  268.9 3.5 all-to-all-start.9
  272.4 7.4 %all-to-all-done.9 = bf16[2,16,2,1,256]{4,2,0,3,1:T(2,128)(2,1)S(1)} async-done(((bf16[2,16,2,1,256]{4,2,0,3,1:T(2,128)(2,1)}), bf16[2,16,2,1,256]{4,2,0,3,1:T(2,128)(2,1)S(1)}, u32[]{:S(2)}, u32[]{:S(2)}) %all-to-all-start.9) | async-done | bytes 32800 | tf_op jit(solution)/shard_map/all_to_all | solution.py:202
  280.7 3.5 all-to-all-start.10
  284.2 7.4 %all-to-all-done.10 = bf16[2,1,2,16,256]{4,2,0,1,3:T(2,128)(2,1)S(1)} async-done(((bf16[2,1,2,16,256]{4,2,0,1,3:T(2,128)(2,1)}), bf16[2,1,2,16,256]{4,2,0,1,3:T(2,128)(2,1)S(1)}, u32[]{:S(2)}, u32[]{:S(2)}) %all-to-all-start.10) | async-done | bytes 32800 | tf_op jit(solution)/shard_map/all_to_all | solution.py:191
  305.2 3.7 all-to-all-start.11
  308.9 2.2 convolution_add_fusion.19
  311.0 5.2 %all-to-all-done.11 = bf16[2,16,2,1,256]{4,2,0,3,1:T(2,128)(2,1)S(1)} async-done(((bf16[2,16,2,1,256]{4,2,0,3,1:T(2,128)(2,1)}), bf16[2,16,2,1,256]{4,2,0,3,1:T(2,128)(2,1)S(1)}, u32[]{:S(2)}, u32[]{:S(2)}) %all-to-all-start.11) | async-done | bytes 32800 | tf_op jit(solution)/shard_map/all_to_all | solution.py:202
  317.2 3.5 all-to-all-start.12
  320.8 7.3 %all-to-all-done.12 = bf16[2,1,2,16,256]{4,2,0,1,3:T(2,128)(2,1)S(1)} async-done(((bf16[2,1,2,16,256]{4,2,0,1,3:T(2,128)(2,1)}), bf16[2,1,2,16,256]{4,2,0,1,3:T(2,128)(2,1)S(1)}, u32[]{:S(2)}, u32[]{:S(2)}) %all-to-all-start.12) | async-done | bytes 32800 | tf_op jit(solution)/shard_map/all_to_all | solution.py:191
  339.6 38.5 %psum.79 = f32[2,1024]{1,0:T(2,128)S(1)} all-reduce(f32[2,1024]{1,0:T(2,128)S(1)} %fusion.164), channel_id=1, replica_groups=mesh['tm'=2,'lat'=16] {'tm','lat'}, use_global_device_ids=true, to_apply=%region_88.89 | all-reduce | flops 2048 | bytes 16384 | tf_op jit(solution)/shard_map/psum | solution.py:207
  378.8 90.0 %all-reduce.4.cloned.1.call-done = (f32[256,384]{1,0:T(8,128)}, f32[384,384]{1,0:T(8,128)}, f32[384,256]{1,0:T(8,128)}) async-done(((f32[256,384]{1,0:T(8,128)}, f32[384,384]{1,0:T(8,128)}, f32[384,256]{1,0:T(8,128)}), (f32[256,384]{1,0:T(8,128)}, f32[384,384]{1,0:T(8,128)}, f32[384,256]{1,0:T(8,128)})) %all-reduce.4.cloned.1.call-update) | async-done | bytes 1376272 | tf_op jit(solution)/shard_map/psum | solution.py:207
  (512 shorter events, 108.9 us)
Async XLA Ops:
  9.2 11.4 %copy-start.37 = (f32[256,384]{1,0:T(8,128)S(1)}, f32[256,384]{1,0:T(8,128)}, u32[]{:S(2)}) copy-start(f32[256,384]{1,0:T(8,128)} %param.26) | copy-start | bytes 1179652
  10.6 9.1 %copy-start.91 = (f32[2,1024]{1,0:T(2,128)S(1)}, f32[2,1024]{1,0:T(2,128)}, u32[]{:S(2)}) copy-start(f32[2,1024]{1,0:T(2,128)} %param.29) | copy-start | bytes 24580
  10.8 9.9 %copy-start.39 = (f32[384,256]{1,0:T(8,128)S(1)}, f32[384,256]{1,0:T(8,128)}, u32[]{:S(2)}) copy-start(f32[384,256]{1,0:T(8,128)} %param.28) | copy-start | bytes 1179652
  11.4 15.8 %all-to-all-start = ((bf16[2,1,2,16,256]{4,2,0,1,3:T(2,128)(2,1)}), bf16[2,1,2,16,256]{4,2,0,1,3:T(2,128)(2,1)S(1)}, u32[]{:S(2)}, u32[]{:S(2)}) async-start(bf16[2,1,2,16,256]{4,2,0,1,3:T(2,128)(2,1)} %copy.194), calls=%async_computation | async-start | bytes 65536 | tf_op jit(solution)/shard_map/all_to_all | solution.py:141
  19.8 73.5 %copy-start.139 = (f32[384]{0:T(512)}, f32[384]{0:T(512)S(1)}, u32[]{:S(2)}) copy-start(f32[384]{0:T(512)S(1)} %get-tuple-element.47) | copy-start | bytes 4612
  19.8 76.8 %copy-start.137 = (f32[384]{0:T(512)}, f32[384]{0:T(512)S(1)}, u32[]{:S(2)}) copy-start(f32[384]{0:T(512)S(1)} %get-tuple-element.45) | copy-start | bytes 4612
  20.6 72.7 %copy-start.24 = (bf16[256,384]{1,0:T(8,128)(2,1)}, bf16[256,384]{1,0:T(8,128)(2,1)S(1)}, u32[]{:S(2)}) copy-start(bf16[256,384]{1,0:T(8,128)(2,1)S(1)} %convert_element_type.413) | copy-start | bytes 589828
  21.8 74.9 %copy-start.21 = (bf16[384,384]{1,0:T(8,128)(2,1)}, bf16[384,384]{1,0:T(8,128)(2,1)S(1)}, u32[]{:S(2)}) copy-start(bf16[384,384]{1,0:T(8,128)(2,1)S(1)} %convert_element_type.415) | copy-start | bytes 884740
  28.0 3.0 copy-start.28
  31.0 4.0 copy-start.4
  31.9 3.2 copy-start.93
  60.6 3.0 copy-start.48
  63.7 4.0 copy-start.6
  64.5 3.2 copy-start.95
  93.4 3.1 copy-start.50
  96.5 3.4 copy-start.8
  96.6 3.2 copy-start.109
  96.6 3.2 copy-start.97
  113.0 3.9 copy-start.123
  113.0 19.9 %all-to-all-start.6 = ((bf16[2,1,2,16,256]{4,2,0,1,3:T(2,128)(2,1)}), bf16[2,1,2,16,256]{4,2,0,1,3:T(2,128)(2,1)S(1)}, u32[]{:S(2)}, u32[]{:S(2)}) async-start(bf16[2,1,2,16,256]{4,2,0,1,3:T(2,128)(2,1)} %copy.216), calls=%async_computation.6 | async-start | bytes 65536 | tf_op jit(solution)/shard_map/all_to_all | solution.py:141
  122.7 2.1 copy-start.11
  127.9 2.1 copy-start.13
  133.3 71.8 %copy-start.87 = (f32[1,2,2,128]{3,1,2,0:T(2,128)}, f32[1,2,2,128]{3,1,2,0:T(2,128)S(1)}, u32[]{:S(2)}) copy-start(f32[1,2,2,128]{3,1,2,0:T(2,128)S(1)} %copy.333) | copy-start | bytes 6148
  135.0 70.1 %copy-start.89 = (f32[512]{0:T(512)}, f32[512]{0:T(512)S(1)}, u32[]{:S(2)}) copy-start(f32[512]{0:T(512)S(1)} %rsqrt.155) | copy-start | bytes 6148
  136.3 3.1 copy-start.52
  139.4 4.4 copy-start.2
  139.5 4.2 copy-start.113
  140.6 3.2 copy-start.99
  208.6 5.5 %copy-start.136 = (f32[2,8]{1,0:T(2,128)S(1)}, f32[2,8]{1,0:T(2,128)}, u32[]{:S(2)}) copy-start(f32[2,8]{1,0:T(2,128)} %get-tuple-element.143) | copy-start | bytes 196
  230.8 3.7 copy-start.128
  230.8 11.0 %all-to-all-start.7 = ((bf16[2,16,2,1,256]{4,2,0,3,1:T(2,128)(2,1)}), bf16[2,16,2,1,256]{4,2,0,3,1:T(2,128)(2,1)S(1)}, u32[]{:S(2)}, u32[]{:S(2)}) async-start(bf16[2,16,2,1,256]{4,2,0,3,1:T(2,128)(2,1)} %copy.228), calls=%async_computation.7 | async-start | bytes 65536 | tf_op jit(solution)/shard_map/all_to_all | solution.py:202
  242.8 10.9 %all-to-all-start.8 = ((bf16[2,1,2,16,256]{4,2,0,1,3:T(2,128)(2,1)}), bf16[2,1,2,16,256]{4,2,0,1,3:T(2,128)(2,1)S(1)}, u32[]{:S(2)}, u32[]{:S(2)}) async-start(bf16[2,1,2,16,256]{4,2,0,1,3:T(2,128)(2,1)} %copy.231), calls=%async_computation.8 | async-start | bytes 65536 | tf_op jit(solution)/shard_map/all_to_all | solution.py:191
  265.1 2.2 copy-start.120
  268.0 23.6 %copy-start.36 = (f32[2,1,256,256]{3,2,0,1:T(8,128)S(1)}, f32[2,1,256,256]{3,2,0,1:T(8,128)}, u32[]{:S(2)}) copy-start(f32[2,1,256,256]{3,2,0,1:T(8,128)} %copy.243) | copy-start | bytes 1572868
  268.9 10.9 %all-to-all-start.9 = ((bf16[2,16,2,1,256]{4,2,0,3,1:T(2,128)(2,1)}), bf16[2,16,2,1,256]{4,2,0,3,1:T(2,128)(2,1)S(1)}, u32[]{:S(2)}, u32[]{:S(2)}) async-start(bf16[2,16,2,1,256]{4,2,0,3,1:T(2,128)(2,1)} %copy.238), calls=%async_computation.9 | async-start | bytes 65536 | tf_op jit(solution)/shard_map/all_to_all | solution.py:202
  280.7 10.9 %all-to-all-start.10 = ((bf16[2,1,2,16,256]{4,2,0,1,3:T(2,128)(2,1)}), bf16[2,1,2,16,256]{4,2,0,1,3:T(2,128)(2,1)S(1)}, u32[]{:S(2)}, u32[]{:S(2)}) async-start(bf16[2,1,2,16,256]{4,2,0,1,3:T(2,128)(2,1)} %copy.241), calls=%async_computation.10 | async-start | bytes 65536 | tf_op jit(solution)/shard_map/all_to_all | solution.py:191
  304.3 4.5 copy-start.49
  305.2 11.0 %all-to-all-start.11 = ((bf16[2,16,2,1,256]{4,2,0,3,1:T(2,128)(2,1)}), bf16[2,16,2,1,256]{4,2,0,3,1:T(2,128)(2,1)S(1)}, u32[]{:S(2)}, u32[]{:S(2)}) async-start(bf16[2,16,2,1,256]{4,2,0,3,1:T(2,128)(2,1)} %copy.248), calls=%async_computation.11 | async-start | bytes 65536 | tf_op jit(solution)/shard_map/all_to_all | solution.py:202
  308.9 19.2 %copy-start.35 = (f32[2,1,256,256]{3,2,0,1:T(8,128)S(1)}, f32[2,1,256,256]{3,2,0,1:T(8,128)}, u32[]{:S(2)}) copy-start(f32[2,1,256,256]{3,2,0,1:T(8,128)} %copy.253) | copy-start | bytes 1572868
  317.2 10.9 %all-to-all-start.12 = ((bf16[2,1,2,16,256]{4,2,0,1,3:T(2,128)(2,1)}), bf16[2,1,2,16,256]{4,2,0,1,3:T(2,128)(2,1)S(1)}, u32[]{:S(2)}, u32[]{:S(2)}) async-start(bf16[2,1,2,16,256]{4,2,0,1,3:T(2,128)(2,1)} %copy.251), calls=%async_computation.12 | async-start | bytes 65536 | tf_op jit(solution)/shard_map/all_to_all | solution.py:191
  320.7 148.0 %all-reduce.4.cloned.1.call-start = ((), (), s32[]{:S(2)}) async-start(), calls=%async_computation.13 | async-start | bytes 2752512 | tf_op jit(solution)/shard_map/psum | solution.py:207
  339.2 137.3 %copy-start.72 = (f32[256,384]{1,0:T(8,128)S(1)}, f32[256,384]{1,0:T(8,128)}, u32[]{:S(2)}) copy-start(f32[256,384]{1,0:T(8,128)} %param.30) | copy-start | bytes 1179652
  468.7 7.7 %copy-start.71 = (f32[256,384]{1,0:T(8,128)S(1)}, f32[256,384]{1,0:T(8,128)}, u32[]{:S(2)}) copy-start(f32[256,384]{1,0:T(8,128)} %param.34) | copy-start | bytes 1179652
  470.5 6.0 %copy-start.38 = (f32[256,384]{1,0:T(8,128)S(1)}, f32[256,384]{1,0:T(8,128)}, u32[]{:S(2)}) copy-start(f32[256,384]{1,0:T(8,128)} %param.26) | copy-start | bytes 1179652
  472.4 3.4 copy-start.129
  472.4 3.4 copy-start.130
  473.1 2.7 copy-start.92
  478.3 2.1 copy-start.70
  (104 other events, 121.1 us)
Sparse Core Ops, SparseCore 0:
  339.3 129.3 all-reduce.3
where the time goes:
time: 499 us; the launch traced here: 491 us
  waiting for transfers between devices  136 us (27%)
  blocking collectives  134 us (27%)
  matrix products  61.3 us (12%)
  local copies, waits for them, and re-layouts  61.2 us (12%)
  other arithmetic  44.3 us (9%)
  starting transfers between devices  33.5 us (7%)
  between operations  20.2 us (4%)
    psum x1, waiting for transfers between devices, per_device(): grads = lax.psum(totals, ('tm', 'lat'))  90 us
    psum x1, blocking collectives, per_device(): num_total, den_total = lax.psum((num_part, den_part), 'lat')  42.5 us
    psum x1, blocking collectives, per_device(): grads = lax.psum(totals, ('tm', 'lat'))  38.5 us
    dot_general x12, matrix products, corrector_forward(): jnp.dot(h_low, weights[k], preferred_element_type=jnp.float32)  31.7 us
    all_to_all x3, blocking collectives, per_device(): lax.all_to_all(coeff, 'lat', split_axis=1, concat_axis=3, tiled=True)  29.9 us
    unnamed x297, local copies, waits for them, and re-layouts  29.6 us
    all_to_all x3, waiting for transfers between devices, per_device(): lax.all_to_all(back_coeff, 'lat', split_axis=3, concat_axis=1, tiled=True)  21.3 us
    all_to_all x2, blocking collectives, to_grid(): lax.all_to_all(sums, 'lat', split_axis=3, concat_axis=1, tiled=True)  20.1 us
  transfers between devices with their start and end apart: 9, of which 8 were waited for; matrix products, arithmetic and copies ran while one was open for 4% of the time, Pallas kernels for 0%

commit v1 on v0

--- a/solution.py
+++ b/solution.py
@@ -187,9 +187,31 @@
             back_coeff = jnp.einsum(
                 "mnr,tmpnc->tmprc", plg, back_spec, preferred_element_type=jnp.float32
             ).astype(jnp.bfloat16)
-            back_tend = fourier_sum(
-                ffw, lax.all_to_all(back_coeff, "lat", split_axis=3, concat_axis=1, tiled=True)
-            )
+
+            def use_modes(work_x):
+                part_next = lax.axis_size("lat")
+                far_arr = lax.axis_index("lat")
+                y_new, o_now = (part_next, far_arr)
+                formed = work_x.shape[3] // y_new
+                outcome_arr = list(work_x.shape)
+                outcome_arr[3] = formed
+                upper = outcome_arr[1]
+                outcome_arr[1] = upper * y_new
+                tmp = jnp.zeros(outcome_arr, work_x.dtype)
+                for src_i in tuple(range(y_new)):
+                    side_arr = lax.dynamic_slice_in_dim(
+                        work_x, (o_now ^ src_i) * formed, formed, axis=3
+                    )
+                    if src_i:
+                        side_arr = lax.ppermute(
+                            side_arr, "lat", [(dev_i, dev_i ^ src_i) for dev_i in range(y_new)]
+                        )
+                    tmp = lax.dynamic_update_slice_in_dim(
+                        tmp, side_arr, (o_now ^ src_i) * upper, axis=1
+                    )
+                return tmp
+
+            back_tend = fourier_sum(ffw, use_modes(back_coeff))
             back_out = back_out + qlocal[None, :, None, None] * back_tend
         back_in, grads = corrector_backward(back_out.reshape(-1, chans), saved, weights, norm_bias)
         totals = tuple((a + b for a, b in zip(totals, grads)))

time: 499 us -> 575 us (1.15)
  starting transfers between devices: 33.5 us -> 106 us
  waiting for transfers between devices: 136 us -> 117 us
  local copies, waits for them, and re-layouts: 61.2 us -> 71.2 us
  other arithmetic: 44.3 us -> 51.9 us
    ppermute x0 -> x45, starting transfers between devices: none -> 79.9 us  [use_modes(): lax.ppermute(side_arr, 'lat', [(dev_i, dev_i ^ src_i) for dev_i in range(...]
    all_to_all x3 -> x0, waiting for transfers between devices: 21.3 us -> none  [per_device(): lax.all_to_all(back_coeff, 'lat', split_axis=3, concat_axis=1, tiled=True)]
    all_to_all x3 -> x0, starting transfers between devices: 10.5 us -> none  [per_device(): lax.all_to_all(back_coeff, 'lat', split_axis=3, concat_axis=1, tiled=True)]
    another operation x0 -> x51, local copies, waits for them, and re-layouts: none -> 7.91 us
    unnamed x297 -> x385, local copies, waits for them, and re-layouts: 29.6 us -> 35.6 us
  transfers between devices with their start and end apart: 9 -> 51, of which waited for: 8 -> 8; matrix products, arithmetic and copies ran while one was open for 4% -> 8% of each run, Pallas kernels for 0% -> 0%
where the time goes in v1:
time: 575 us; the launch traced here: 566 us
  blocking collectives  135 us (23%)
  waiting for transfers between devices  117 us (20%)
  starting transfers between devices  106 us (18%)
  local copies, waits for them, and re-layouts  71.2 us (12%)
  matrix products  64.6 us (11%)
  other arithmetic  51.9 us (9%)
  between operations  20.9 us (4%)
    psum x1, waiting for transfers between devices, per_device(): grads = lax.psum(totals, ('tm', 'lat'))  92.1 us
    ppermute x45, starting transfers between devices, use_modes(): lax.ppermute(side_arr, 'lat', [(dev_i, dev_i ^ src_i) for dev_i in range(...  79.9 us
    psum x1, blocking collectives, per_device(): num_total, den_total = lax.psum((num_part, den_part), 'lat')  42.6 us
    psum x1, blocking collectives, per_device(): grads = lax.psum(totals, ('tm', 'lat'))  39.6 us
    unnamed x385, local copies, waits for them, and re-layouts  35.6 us
    dot_general x12, matrix products, corrector_forward(): jnp.dot(h_low, weights[k], preferred_element_type=jnp.float32)  31.7 us
    all_to_all x3, blocking collectives, per_device(): lax.all_to_all(coeff, 'lat', split_axis=1, concat_axis=3, tiled=True)  29.9 us
    all_to_all x2, blocking collectives, to_grid(): lax.all_to_all(sums, 'lat', split_axis=3, concat_axis=1, tiled=True)  20.1 us
  transfers between devices with their start and end apart: 51, of which 8 were waited for; matrix products, arithmetic and copies ran while one was open for 8% of the time, Pallas kernels for 0%

profile of v1, /device:TPU:0, one launch (start us, length us, event | category | flops | bytes accessed | tf_op | source)
XLA Modules:
  0.0 566.5 jit_solution(8622951941645543158)
XLA Ops:
  11.4 8.3 %all-to-all-start = ((bf16[2,1,2,16,256]{4,2,0,1,3:T(2,128)(2,1)}), bf16[2,1,2,16,256]{4,2,0,1,3:T(2,128)(2,1)S(1)}, u32[]{:S(2)}, u32[]{:S(2)}) async-start(bf16[2,1,2,16,256]{4,2,0,1,3:T(2,128)(2,1)} %copy.278), calls=%async_computation | async-start | bytes 65536 | tf_op jit(solution)/shard_map/all_to_all | solution.py:141
  21.8 5.3 all-to-all-done
  28.0 3.0 fusion.208
  31.9 3.2 fusion.206
  37.8 10.0 %all_to_all.170 = bf16[2,16,2,1,256]{4,2,0,3,1:T(2,128)(2,1)S(1)} all-to-all(bf16[2,16,2,1,256]{4,2,0,3,1:T(2,128)(2,1)S(1)} %copy.282), channel_id=1, replica_groups=mesh['tm'=2,'lat'=16] {'lat'}, dimensions={1} | all-to-all | bytes 65536 | tf_op jit(solution)/shard_map/all_to_all | solution.py:169
  48.1 10.1 %all_to_all.171 = bf16[2,1,2,16,256]{4,2,0,1,3:T(2,128)(2,1)S(1)} all-to-all(bf16[2,1,2,16,256]{4,2,0,1,3:T(2,128)(2,1)S(1)} %copy.286), channel_id=1, replica_groups=mesh['tm'=2,'lat'=16] {'lat'}, dimensions={3} | all-to-all | bytes 65536 | tf_op jit(solution)/shard_map/all_to_all | solution.py:141
  60.6 3.0 fusion.204
  64.5 3.2 fusion.202
  70.5 10.0 %all_to_all.172 = bf16[2,16,2,1,256]{4,2,0,3,1:T(2,128)(2,1)S(1)} all-to-all(bf16[2,16,2,1,256]{4,2,0,3,1:T(2,128)(2,1)S(1)} %copy.290), channel_id=1, replica_groups=mesh['tm'=2,'lat'=16] {'lat'}, dimensions={1} | all-to-all | bytes 65536 | tf_op jit(solution)/shard_map/all_to_all | solution.py:169
  80.8 10.0 %all_to_all.173 = bf16[2,1,2,16,256]{4,2,0,1,3:T(2,128)(2,1)S(1)} all-to-all(bf16[2,1,2,16,256]{4,2,0,1,3:T(2,128)(2,1)S(1)} %copy.293), channel_id=1, replica_groups=mesh['tm'=2,'lat'=16] {'lat'}, dimensions={3} | all-to-all | bytes 65536 | tf_op jit(solution)/shard_map/all_to_all | solution.py:141
  93.4 3.1 fusion.200
  96.6 3.2 fusion.198
  102.0 10.0 %all_to_all.174 = bf16[2,16,2,1,256]{4,2,0,3,1:T(2,128)(2,1)S(1)} all-to-all(bf16[2,16,2,1,256]{4,2,0,3,1:T(2,128)(2,1)S(1)} %copy.297), channel_id=1, replica_groups=mesh['tm'=2,'lat'=16] {'lat'}, dimensions={1} | all-to-all | bytes 65536 | tf_op jit(solution)/shard_map/all_to_all | solution.py:169
  113.0 3.8 all-to-all-start.6
  123.3 2.1 copy.289
  136.8 3.1 fusion.196
  141.1 3.2 fusion.194
  151.6 42.6 %all-reduce.1 = (f32[1,2,8]{2,1,0:T(2,128)S(1)}, f32[1,2,8]{2,1,0:T(2,128)S(1)}, f32[1,2,8]{2,1,0:T(2,128)S(1)}, f32[1,2,8]{2,1,0:T(2,128)S(1)}, f32[2,8]{1,0:T(2,128)S(1)}) all-reduce(f32[1,2,8]{2,1,0:T(2,128)S(1)} %bitcast.827, f32[1,2,8]{2,1,0:T(2,128)S(1)} %bitcast.828, ...), channel_id=1, replica_groups=mesh['tm'=2,'lat'=16] {'lat'}, use_global_device_ids=true, to_apply=%region_31.32 | all-reduce | flops 80 | bytes 640 | tf_op jit(solution)/shard_map/psum | solution.py:163
  214.6 4.0 all-to-all-start.7
  219.2 6.3 %all-to-all-done.7 = bf16[2,16,2,1,256]{4,2,0,3,1:T(2,128)(2,1)S(1)} async-done(((bf16[2,16,2,1,256]{4,2,0,3,1:T(2,128)(2,1)}), bf16[2,16,2,1,256]{4,2,0,3,1:T(2,128)(2,1)S(1)}, u32[]{:S(2)}, u32[]{:S(2)}) %all-to-all-start.7) | async-done | bytes 32800 | tf_op jit(solution)/shard_map/all_to_all | solution.py:224
  227.7 2.3 collective-permute-start.2
  237.6 3.2 collective-permute-start.6
  241.5 2.5 collective-permute-start.8
  245.9 3.0 psum.75
  254.5 4.0 collective-permute-start.10
  259.2 3.3 collective-permute-start.12
  263.1 4.9 collective-permute-start.14
  278.3 2.5 convert_reduce_fusion.10
  295.5 3.5 all-to-all-start.8
  301.1 5.3 all-to-all-done.8
  308.1 2.3 collective-permute-start.17
  312.6 2.2 convolution_add_fusion.20
  315.4 3.2 collective-permute-start.21
  319.3 2.4 collective-permute-start.23
  323.0 4.1 collective-permute-start.25
  327.8 3.3 collective-permute-start.27
  331.6 4.9 collective-permute-start.29
  353.7 6.3 %all-to-all-start.9 = ((bf16[2,16,2,1,256]{4,2,0,3,1:T(2,128)(2,1)}), bf16[2,16,2,1,256]{4,2,0,3,1:T(2,128)(2,1)S(1)}, u32[]{:S(2)}, u32[]{:S(2)}) async-start(bf16[2,16,2,1,256]{4,2,0,3,1:T(2,128)(2,1)} %copy.358), calls=%async_computation.9 | async-start | bytes 65536 | tf_op jit(solution)/shard_map/all_to_all | solution.py:224
  360.1 2.4 convolution_add_fusion.9
  362.5 4.9 all-to-all-done.9
  369.1 2.3 collective-permute-start.32
  375.6 3.2 collective-permute-start.36
  379.4 2.4 collective-permute-start.38
  383.6 4.1 collective-permute-start.40
  388.4 3.2 collective-permute-start.42
  392.3 4.9 collective-permute-start.44
  412.1 39.6 %psum.79 = f32[2,1024]{1,0:T(2,128)S(1)} all-reduce(f32[2,1024]{1,0:T(2,128)S(1)} %fusion.155), channel_id=1, replica_groups=mesh['tm'=2,'lat'=16] {'tm','lat'}, use_global_device_ids=true, to_apply=%region_88.89 | all-reduce | flops 2048 | bytes 16384 | tf_op jit(solution)/shard_map/psum | solution.py:229
  452.4 92.1 %all-reduce.4.cloned.1.call-done = (f32[256,384]{1,0:T(8,128)}, f32[384,384]{1,0:T(8,128)}, f32[384,256]{1,0:T(8,128)}) async-done(((f32[256,384]{1,0:T(8,128)}, f32[384,384]{1,0:T(8,128)}, f32[384,256]{1,0:T(8,128)}), (f32[256,384]{1,0:T(8,128)}, f32[384,384]{1,0:T(8,128)}, f32[384,256]{1,0:T(8,128)})) %all-reduce.4.cloned.1.call-update) | async-done | bytes 1376272 | tf_op jit(solution)/shard_map/psum | solution.py:229
  (779 shorter events, 175.9 us)
Async XLA Ops:
  11.4 15.8 %all-to-all-start = ((bf16[2,1,2,16,256]{4,2,0,1,3:T(2,128)(2,1)}), bf16[2,1,2,16,256]{4,2,0,1,3:T(2,128)(2,1)S(1)}, u32[]{:S(2)}, u32[]{:S(2)}) async-start(bf16[2,1,2,16,256]{4,2,0,1,3:T(2,128)(2,1)} %copy.278), calls=%async_computation | async-start | bytes 65536 | tf_op jit(solution)/shard_map/all_to_all | solution.py:141
  113.0 20.5 %all-to-all-start.6 = ((bf16[2,1,2,16,256]{4,2,0,1,3:T(2,128)(2,1)}), bf16[2,1,2,16,256]{4,2,0,1,3:T(2,128)(2,1)S(1)}, u32[]{:S(2)}, u32[]{:S(2)}) async-start(bf16[2,1,2,16,256]{4,2,0,1,3:T(2,128)(2,1)} %copy.300), calls=%async_computation.6 | async-start | bytes 65536 | tf_op jit(solution)/shard_map/all_to_all | solution.py:141
  214.6 10.9 %all-to-all-start.7 = ((bf16[2,16,2,1,256]{4,2,0,3,1:T(2,128)(2,1)}), bf16[2,16,2,1,256]{4,2,0,3,1:T(2,128)(2,1)S(1)}, u32[]{:S(2)}, u32[]{:S(2)}) async-start(bf16[2,16,2,1,256]{4,2,0,3,1:T(2,128)(2,1)} %copy.312), calls=%async_computation.7 | async-start | bytes 65536 | tf_op jit(solution)/shard_map/all_to_all | solution.py:224
  226.5 10.6 %collective-permute-start = (bf16[2,1,2,1,256]{4,2,0,3,1:T(2,128)(2,1)S(1)}, bf16[2,1,2,1,256]{4,2,0,3,1:T(2,128)(2,1)S(1)}, u32[]{:S(2)}, u32[]{:S(2)}) collective-permute-start(bf16[2,1,2,1,256]{4,2,0,3,1:T(2,128)(2,1)S(1)} %bitcast.897), channel_id=1, source_target_pairs={{0,1},{1,0},{2,3},{3,2},{4,5},{5,4},{6,7},{7,6},{8,9},{9,8},{10,11... | collective-permute-start | bytes 6152 | tf_op jit(solution)/shard_map/ppermute | solution.py:206
  227.3 10.3 %collective-permute-start.1 = (bf16[2,1,2,1,256]{4,2,0,3,1:T(2,128)(2,1)S(1)}, bf16[2,1,2,1,256]{4,2,0,3,1:T(2,128)(2,1)S(1)}, u32[]{:S(2)}, u32[]{:S(2)}) collective-permute-start(bf16[2,1,2,1,256]{4,2,0,3,1:T(2,128)(2,1)S(1)} %bitcast.894), channel_id=1, source_target_pairs={{0,2},{1,3},{2,0},{3,1},{4,6},{5,7},{6,4},{7,5},{8,10},{9,11},{10,... | collective-permute-start | bytes 6152 | tf_op jit(solution)/shard_map/ppermute | solution.py:206
  227.7 13.1 %collective-permute-start.2 = (bf16[2,1,2,1,256]{4,2,0,3,1:T(2,128)(2,1)S(1)}, bf16[2,1,2,1,256]{4,2,0,3,1:T(2,128)(2,1)S(1)}, u32[]{:S(2)}, u32[]{:S(2)}) collective-permute-start(bf16[2,1,2,1,256]{4,2,0,3,1:T(2,128)(2,1)S(1)} %bitcast.889), channel_id=1, source_target_pairs={{0,3},{1,2},{2,1},{3,0},{4,7},{5,6},{6,5},{7,4},{8,11},{9,10},{10,... | collective-permute-start | bytes 6152 | tf_op jit(solution)/shard_map/ppermute | solution.py:206
  230.1 11.4 %collective-permute-start.3 = (bf16[2,1,2,1,256]{4,2,0,3,1:T(2,128)(2,1)S(1)}, bf16[2,1,2,1,256]{4,2,0,3,1:T(2,128)(2,1)S(1)}, u32[]{:S(2)}, u32[]{:S(2)}) collective-permute-start(bf16[2,1,2,1,256]{4,2,0,3,1:T(2,128)(2,1)S(1)} %bitcast.875), channel_id=1, source_target_pairs={{0,4},{1,5},{2,6},{3,7},{4,0},{5,1},{6,2},{7,3},{8,12},{9,13},{10,... | collective-permute-start | bytes 6152 | tf_op jit(solution)/shard_map/ppermute | solution.py:206
  230.7 13.3 %collective-permute-start.4 = (bf16[2,1,2,1,256]{4,2,0,3,1:T(2,128)(2,1)S(1)}, bf16[2,1,2,1,256]{4,2,0,3,1:T(2,128)(2,1)S(1)}, u32[]{:S(2)}, u32[]{:S(2)}) collective-permute-start(bf16[2,1,2,1,256]{4,2,0,3,1:T(2,128)(2,1)S(1)} %bitcast.867), channel_id=1, source_target_pairs={{0,5},{1,4},{2,7},{3,6},{4,1},{5,0},{6,3},{7,2},{8,13},{9,12},{10,... | collective-permute-start | bytes 6152 | tf_op jit(solution)/shard_map/ppermute | solution.py:206
  237.1 17.4 %collective-permute-start.5 = (bf16[2,1,2,1,256]{4,2,0,3,1:T(2,128)(2,1)}, bf16[2,1,2,1,256]{4,2,0,3,1:T(2,128)(2,1)}, u32[]{:S(2)}, u32[]{:S(2)}) collective-permute-start(bf16[2,1,2,1,256]{4,2,0,3,1:T(2,128)(2,1)} %bitcast.751), channel_id=1, source_target_pairs={{0,6},{1,7},{2,4},{3,5},{4,2},{5,3},{6,0},{7,1},{8,14},{9,15},{10,... | collective-permute-start | bytes 6152 | tf_op jit(solution)/shard_map/ppermute | solution.py:206
  237.6 20.9 %collective-permute-start.6 = (bf16[2,1,2,1,256]{4,2,0,3,1:T(2,128)(2,1)}, bf16[2,1,2,1,256]{4,2,0,3,1:T(2,128)(2,1)}, u32[]{:S(2)}, u32[]{:S(2)}) collective-permute-start(bf16[2,1,2,1,256]{4,2,0,3,1:T(2,128)(2,1)} %bitcast.750), channel_id=1, source_target_pairs={{0,7},{1,6},{2,5},{3,4},{4,3},{5,2},{6,1},{7,0},{8,15},{9,14},{10,... | collective-permute-start | bytes 6152 | tf_op jit(solution)/shard_map/ppermute | solution.py:206
  240.8 18.4 %collective-permute-start.7 = (bf16[2,1,2,1,256]{4,2,0,3,1:T(2,128)(2,1)}, bf16[2,1,2,1,256]{4,2,0,3,1:T(2,128)(2,1)}, u32[]{:S(2)}, u32[]{:S(2)}) collective-permute-start(bf16[2,1,2,1,256]{4,2,0,3,1:T(2,128)(2,1)} %bitcast.749), channel_id=1, source_target_pairs={{0,8},{1,9},{2,10},{3,11},{4,12},{5,13},{6,14},{7,15},{8,0},{9,1},... | collective-permute-start | bytes 6152 | tf_op jit(solution)/shard_map/ppermute | solution.py:206
  241.5 21.0 %collective-permute-start.8 = (bf16[2,1,2,1,256]{4,2,0,3,1:T(2,128)(2,1)}, bf16[2,1,2,1,256]{4,2,0,3,1:T(2,128)(2,1)}, u32[]{:S(2)}, u32[]{:S(2)}) collective-permute-start(bf16[2,1,2,1,256]{4,2,0,3,1:T(2,128)(2,1)} %bitcast.748), channel_id=1, source_target_pairs={{0,9},{1,8},{2,11},{3,10},{4,13},{5,12},{6,15},{7,14},{8,1},{9,0},... | collective-permute-start | bytes 6152 | tf_op jit(solution)/shard_map/ppermute | solution.py:206
  244.0 19.1 %collective-permute-start.9 = (bf16[2,1,2,1,256]{4,2,0,3,1:T(2,128)(2,1)}, bf16[2,1,2,1,256]{4,2,0,3,1:T(2,128)(2,1)}, u32[]{:S(2)}, u32[]{:S(2)}) collective-permute-start(bf16[2,1,2,1,256]{4,2,0,3,1:T(2,128)(2,1)} %bitcast.747), channel_id=1, source_target_pairs={{0,10},{1,11},{2,8},{3,9},{4,14},{5,15},{6,12},{7,13},{8,2},{9,3},... | collective-permute-start | bytes 6152 | tf_op jit(solution)/shard_map/ppermute | solution.py:206
  254.5 19.7 %collective-permute-start.10 = (bf16[2,1,2,1,256]{4,2,0,3,1:T(2,128)(2,1)}, bf16[2,1,2,1,256]{4,2,0,3,1:T(2,128)(2,1)}, u32[]{:S(2)}, u32[]{:S(2)}) collective-permute-start(bf16[2,1,2,1,256]{4,2,0,3,1:T(2,128)(2,1)} %bitcast.746), channel_id=1, source_target_pairs={{0,11},{1,10},{2,9},{3,8},{4,15},{5,14},{6,13},{7,12},{8,3},{9,2},... | collective-permute-start | bytes 6152 | tf_op jit(solution)/shard_map/ppermute | solution.py:206
  258.5 16.4 %collective-permute-start.11 = (bf16[2,1,2,1,256]{4,2,0,3,1:T(2,128)(2,1)}, bf16[2,1,2,1,256]{4,2,0,3,1:T(2,128)(2,1)}, u32[]{:S(2)}, u32[]{:S(2)}) collective-permute-start(bf16[2,1,2,1,256]{4,2,0,3,1:T(2,128)(2,1)} %bitcast.745), channel_id=1, source_target_pairs={{0,12},{1,13},{2,14},{3,15},{4,8},{5,9},{6,10},{7,11},{8,4},{9,5},... | collective-permute-start | bytes 6152 | tf_op jit(solution)/shard_map/ppermute | solution.py:206
  259.2 16.4 %collective-permute-start.12 = (bf16[2,1,2,1,256]{4,2,0,3,1:T(2,128)(2,1)}, bf16[2,1,2,1,256]{4,2,0,3,1:T(2,128)(2,1)}, u32[]{:S(2)}, u32[]{:S(2)}) collective-permute-start(bf16[2,1,2,1,256]{4,2,0,3,1:T(2,128)(2,1)} %bitcast.744), channel_id=1, source_target_pairs={{0,13},{1,12},{2,15},{3,14},{4,9},{5,8},{6,11},{7,10},{8,5},{9,4},... | collective-permute-start | bytes 6152 | tf_op jit(solution)/shard_map/ppermute | solution.py:206
  262.5 13.8 %collective-permute-start.13 = (bf16[2,1,2,1,256]{4,2,0,3,1:T(2,128)(2,1)}, bf16[2,1,2,1,256]{4,2,0,3,1:T(2,128)(2,1)}, u32[]{:S(2)}, u32[]{:S(2)}) collective-permute-start(bf16[2,1,2,1,256]{4,2,0,3,1:T(2,128)(2,1)} %bitcast.743), channel_id=1, source_target_pairs={{0,14},{1,15},{2,12},{3,13},{4,10},{5,11},{6,8},{7,9},{8,6},{9,7},... | collective-permute-start | bytes 6152 | tf_op jit(solution)/shard_map/ppermute | solution.py:206
  263.1 13.9 %collective-permute-start.14 = (bf16[2,1,2,1,256]{4,2,0,3,1:T(2,128)(2,1)}, bf16[2,1,2,1,256]{4,2,0,3,1:T(2,128)(2,1)}, u32[]{:S(2)}, u32[]{:S(2)}) collective-permute-start(bf16[2,1,2,1,256]{4,2,0,3,1:T(2,128)(2,1)} %bitcast.742), channel_id=1, source_target_pairs={{0,15},{1,14},{2,13},{3,12},{4,11},{5,10},{6,9},{7,8},{8,7},{9,6},... | collective-permute-start | bytes 6152 | tf_op jit(solution)/shard_map/ppermute | solution.py:206
  295.5 10.9 %all-to-all-start.8 = ((bf16[2,16,2,1,256]{4,2,0,3,1:T(2,128)(2,1)}), bf16[2,16,2,1,256]{4,2,0,3,1:T(2,128)(2,1)S(1)}, u32[]{:S(2)}, u32[]{:S(2)}) async-start(bf16[2,16,2,1,256]{4,2,0,3,1:T(2,128)(2,1)} %copy.335), calls=%async_computation.8 | async-start | bytes 65536 | tf_op jit(solution)/shard_map/all_to_all | solution.py:224
  306.9 7.9 %collective-permute-start.15 = (bf16[2,1,2,1,256]{4,2,0,3,1:T(2,128)(2,1)S(1)}, bf16[2,1,2,1,256]{4,2,0,3,1:T(2,128)(2,1)S(1)}, u32[]{:S(2)}, u32[]{:S(2)}) collective-permute-start(bf16[2,1,2,1,256]{4,2,0,3,1:T(2,128)(2,1)S(1)} %bitcast.899), channel_id=1, source_target_pairs={{0,1},{1,0},{2,3},{3,2},{4,5},{5,4},{6,7},{7,6},{8,9},{9,8},{10,11... | collective-permute-start | bytes 6152 | tf_op jit(solution)/shard_map/ppermute | solution.py:206
  307.7 7.8 %collective-permute-start.16 = (bf16[2,1,2,1,256]{4,2,0,3,1:T(2,128)(2,1)S(1)}, bf16[2,1,2,1,256]{4,2,0,3,1:T(2,128)(2,1)S(1)}, u32[]{:S(2)}, u32[]{:S(2)}) collective-permute-start(bf16[2,1,2,1,256]{4,2,0,3,1:T(2,128)(2,1)S(1)} %bitcast.896), channel_id=1, source_target_pairs={{0,2},{1,3},{2,0},{3,1},{4,6},{5,7},{6,4},{7,5},{8,10},{9,11},{10,... | collective-permute-start | bytes 6152 | tf_op jit(solution)/shard_map/ppermute | solution.py:206
  308.1 10.5 %collective-permute-start.17 = (bf16[2,1,2,1,256]{4,2,0,3,1:T(2,128)(2,1)S(1)}, bf16[2,1,2,1,256]{4,2,0,3,1:T(2,128)(2,1)S(1)}, u32[]{:S(2)}, u32[]{:S(2)}) collective-permute-start(bf16[2,1,2,1,256]{4,2,0,3,1:T(2,128)(2,1)S(1)} %bitcast.892), channel_id=1, source_target_pairs={{0,3},{1,2},{2,1},{3,0},{4,7},{5,6},{6,5},{7,4},{8,11},{9,10},{10,... | collective-permute-start | bytes 6152 | tf_op jit(solution)/shard_map/ppermute | solution.py:206
  310.4 8.8 %collective-permute-start.18 = (bf16[2,1,2,1,256]{4,2,0,3,1:T(2,128)(2,1)S(1)}, bf16[2,1,2,1,256]{4,2,0,3,1:T(2,128)(2,1)S(1)}, u32[]{:S(2)}, u32[]{:S(2)}) collective-permute-start(bf16[2,1,2,1,256]{4,2,0,3,1:T(2,128)(2,1)S(1)} %bitcast.882), channel_id=1, source_target_pairs={{0,4},{1,5},{2,6},{3,7},{4,0},{5,1},{6,2},{7,3},{8,12},{9,13},{10,... | collective-permute-start | bytes 6152 | tf_op jit(solution)/shard_map/ppermute | solution.py:206
  311.1 10.6 %collective-permute-start.19 = (bf16[2,1,2,1,256]{4,2,0,3,1:T(2,128)(2,1)S(1)}, bf16[2,1,2,1,256]{4,2,0,3,1:T(2,128)(2,1)S(1)}, u32[]{:S(2)}, u32[]{:S(2)}) collective-permute-start(bf16[2,1,2,1,256]{4,2,0,3,1:T(2,128)(2,1)S(1)} %bitcast.870), channel_id=1, source_target_pairs={{0,5},{1,4},{2,7},{3,6},{4,1},{5,0},{6,3},{7,2},{8,13},{9,12},{10,... | collective-permute-start | bytes 6152 | tf_op jit(solution)/shard_map/ppermute | solution.py:206
  314.8 8.2 %collective-permute-start.20 = (bf16[2,1,2,1,256]{4,2,0,3,1:T(2,128)(2,1)S(1)}, bf16[2,1,2,1,256]{4,2,0,3,1:T(2,128)(2,1)S(1)}, u32[]{:S(2)}, u32[]{:S(2)}) collective-permute-start(bf16[2,1,2,1,256]{4,2,0,3,1:T(2,128)(2,1)S(1)} %bitcast.890), channel_id=1, source_target_pairs={{0,6},{1,7},{2,4},{3,5},{4,2},{5,3},{6,0},{7,1},{8,14},{9,15},{10,... | collective-permute-start | bytes 6152 | tf_op jit(solution)/shard_map/ppermute | solution.py:206
  315.4 11.7 %collective-permute-start.21 = (bf16[2,1,2,1,256]{4,2,0,3,1:T(2,128)(2,1)S(1)}, bf16[2,1,2,1,256]{4,2,0,3,1:T(2,128)(2,1)S(1)}, u32[]{:S(2)}, u32[]{:S(2)}) collective-permute-start(bf16[2,1,2,1,256]{4,2,0,3,1:T(2,128)(2,1)S(1)} %bitcast.878), channel_id=1, source_target_pairs={{0,7},{1,6},{2,5},{3,4},{4,3},{5,2},{6,1},{7,0},{8,15},{9,14},{10,... | collective-permute-start | bytes 6152 | tf_op jit(solution)/shard_map/ppermute | solution.py:206
  318.6 9.2 %collective-permute-start.22 = (bf16[2,1,2,1,256]{4,2,0,3,1:T(2,128)(2,1)S(1)}, bf16[2,1,2,1,256]{4,2,0,3,1:T(2,128)(2,1)S(1)}, u32[]{:S(2)}, u32[]{:S(2)}) collective-permute-start(bf16[2,1,2,1,256]{4,2,0,3,1:T(2,128)(2,1)S(1)} %bitcast.868), channel_id=1, source_target_pairs={{0,8},{1,9},{2,10},{3,11},{4,12},{5,13},{6,14},{7,15},{8,0},{9,1},... | collective-permute-start | bytes 6152 | tf_op jit(solution)/shard_map/ppermute | solution.py:206
  319.3 11.8 %collective-permute-start.23 = (bf16[2,1,2,1,256]{4,2,0,3,1:T(2,128)(2,1)S(1)}, bf16[2,1,2,1,256]{4,2,0,3,1:T(2,128)(2,1)S(1)}, u32[]{:S(2)}, u32[]{:S(2)}) collective-permute-start(bf16[2,1,2,1,256]{4,2,0,3,1:T(2,128)(2,1)S(1)} %bitcast.861), channel_id=1, source_target_pairs={{0,9},{1,8},{2,11},{3,10},{4,13},{5,12},{6,15},{7,14},{8,1},{9,0},... | collective-permute-start | bytes 6152 | tf_op jit(solution)/shard_map/ppermute | solution.py:206
  321.7 10.0 %collective-permute-start.24 = (bf16[2,1,2,1,256]{4,2,0,3,1:T(2,128)(2,1)S(1)}, bf16[2,1,2,1,256]{4,2,0,3,1:T(2,128)(2,1)S(1)}, u32[]{:S(2)}, u32[]{:S(2)}) collective-permute-start(bf16[2,1,2,1,256]{4,2,0,3,1:T(2,128)(2,1)S(1)} %bitcast.854), channel_id=1, source_target_pairs={{0,10},{1,11},{2,8},{3,9},{4,14},{5,15},{6,12},{7,13},{8,2},{9,3},... | collective-permute-start | bytes 6152 | tf_op jit(solution)/shard_map/ppermute | solution.py:206
  323.0 15.1 %collective-permute-start.25 = (bf16[2,1,2,1,256]{4,2,0,3,1:T(2,128)(2,1)S(1)}, bf16[2,1,2,1,256]{4,2,0,3,1:T(2,128)(2,1)S(1)}, u32[]{:S(2)}, u32[]{:S(2)}) collective-permute-start(bf16[2,1,2,1,256]{4,2,0,3,1:T(2,128)(2,1)S(1)} %bitcast.873), channel_id=1, source_target_pairs={{0,11},{1,10},{2,9},{3,8},{4,15},{5,14},{6,13},{7,12},{8,3},{9,2},... | collective-permute-start | bytes 6152 | tf_op jit(solution)/shard_map/ppermute | solution.py:206
  327.1 11.0 %collective-permute-start.26 = (bf16[2,1,2,1,256]{4,2,0,3,1:T(2,128)(2,1)S(1)}, bf16[2,1,2,1,256]{4,2,0,3,1:T(2,128)(2,1)S(1)}, u32[]{:S(2)}, u32[]{:S(2)}) collective-permute-start(bf16[2,1,2,1,256]{4,2,0,3,1:T(2,128)(2,1)S(1)} %bitcast.866), channel_id=1, source_target_pairs={{0,12},{1,13},{2,14},{3,15},{4,8},{5,9},{6,10},{7,11},{8,4},{9,5},... | collective-permute-start | bytes 6152 | tf_op jit(solution)/shard_map/ppermute | solution.py:206
  327.8 10.3 %collective-permute-start.27 = (bf16[2,1,2,1,256]{4,2,0,3,1:T(2,128)(2,1)S(1)}, bf16[2,1,2,1,256]{4,2,0,3,1:T(2,128)(2,1)S(1)}, u32[]{:S(2)}, u32[]{:S(2)}) collective-permute-start(bf16[2,1,2,1,256]{4,2,0,3,1:T(2,128)(2,1)S(1)} %bitcast.860), channel_id=1, source_target_pairs={{0,13},{1,12},{2,15},{3,14},{4,9},{5,8},{6,11},{7,10},{8,5},{9,4},... | collective-permute-start | bytes 6152 | tf_op jit(solution)/shard_map/ppermute | solution.py:206
  331.6 7.2 %collective-permute-start.29 = (bf16[2,1,2,1,256]{4,2,0,3,1:T(2,128)(2,1)S(1)}, bf16[2,1,2,1,256]{4,2,0,3,1:T(2,128)(2,1)S(1)}, u32[]{:S(2)}, u32[]{:S(2)}) collective-permute-start(bf16[2,1,2,1,256]{4,2,0,3,1:T(2,128)(2,1)S(1)} %bitcast.849), channel_id=1, source_target_pairs={{0,15},{1,14},{2,13},{3,12},{4,11},{5,10},{6,9},{7,8},{8,7},{9,6},... | collective-permute-start | bytes 6152 | tf_op jit(solution)/shard_map/ppermute | solution.py:206
  353.7 13.7 %all-to-all-start.9 = ((bf16[2,16,2,1,256]{4,2,0,3,1:T(2,128)(2,1)}), bf16[2,16,2,1,256]{4,2,0,3,1:T(2,128)(2,1)S(1)}, u32[]{:S(2)}, u32[]{:S(2)}) async-start(bf16[2,16,2,1,256]{4,2,0,3,1:T(2,128)(2,1)} %copy.358), calls=%async_computation.9 | async-start | bytes 65536 | tf_op jit(solution)/shard_map/all_to_all | solution.py:224
  360.0 184.4 %all-reduce.4.cloned.1.call-start = ((), (), s32[]{:S(2)}) async-start(), calls=%async_computation.10 | async-start | bytes 2752512 | tf_op jit(solution)/shard_map/psum | solution.py:229
  367.9 7.1 %collective-permute-start.30 = (bf16[2,1,2,1,256]{4,2,0,3,1:T(2,128)(2,1)S(1)}, bf16[2,1,2,1,256]{4,2,0,3,1:T(2,128)(2,1)S(1)}, u32[]{:S(2)}, u32[]{:S(2)}) collective-permute-start(bf16[2,1,2,1,256]{4,2,0,3,1:T(2,128)(2,1)S(1)} %bitcast.898), channel_id=1, source_target_pairs={{0,1},{1,0},{2,3},{3,2},{4,5},{5,4},{6,7},{7,6},{8,9},{9,8},{10,11... | collective-permute-start | bytes 6152 | tf_op jit(solution)/shard_map/ppermute | solution.py:206
  369.1 9.6 %collective-permute-start.32 = (bf16[2,1,2,1,256]{4,2,0,3,1:T(2,128)(2,1)S(1)}, bf16[2,1,2,1,256]{4,2,0,3,1:T(2,128)(2,1)S(1)}, u32[]{:S(2)}, u32[]{:S(2)}) collective-permute-start(bf16[2,1,2,1,256]{4,2,0,3,1:T(2,128)(2,1)S(1)} %bitcast.891), channel_id=1, source_target_pairs={{0,3},{1,2},{2,1},{3,0},{4,7},{5,6},{6,5},{7,4},{8,11},{9,10},{10,... | collective-permute-start | bytes 6152 | tf_op jit(solution)/shard_map/ppermute | solution.py:206
  371.5 8.0 %collective-permute-start.33 = (bf16[2,1,2,1,256]{4,2,0,3,1:T(2,128)(2,1)S(1)}, bf16[2,1,2,1,256]{4,2,0,3,1:T(2,128)(2,1)S(1)}, u32[]{:S(2)}, u32[]{:S(2)}) collective-permute-start(bf16[2,1,2,1,256]{4,2,0,3,1:T(2,128)(2,1)S(1)} %bitcast.880), channel_id=1, source_target_pairs={{0,4},{1,5},{2,6},{3,7},{4,0},{5,1},{6,2},{7,3},{8,12},{9,13},{10,... | collective-permute-start | bytes 6152 | tf_op jit(solution)/shard_map/ppermute | solution.py:206
  372.1 9.8 %collective-permute-start.34 = (bf16[2,1,2,1,256]{4,2,0,3,1:T(2,128)(2,1)S(1)}, bf16[2,1,2,1,256]{4,2,0,3,1:T(2,128)(2,1)S(1)}, u32[]{:S(2)}, u32[]{:S(2)}) collective-permute-start(bf16[2,1,2,1,256]{4,2,0,3,1:T(2,128)(2,1)S(1)} %bitcast.869), channel_id=1, source_target_pairs={{0,5},{1,4},{2,7},{3,6},{4,1},{5,0},{6,3},{7,2},{8,13},{9,12},{10,... | collective-permute-start | bytes 6152 | tf_op jit(solution)/shard_map/ppermute | solution.py:206
  375.0 8.6 %collective-permute-start.35 = (bf16[2,1,2,1,256]{4,2,0,3,1:T(2,128)(2,1)S(1)}, bf16[2,1,2,1,256]{4,2,0,3,1:T(2,128)(2,1)S(1)}, u32[]{:S(2)}, u32[]{:S(2)}) collective-permute-start(bf16[2,1,2,1,256]{4,2,0,3,1:T(2,128)(2,1)S(1)} %bitcast.893), channel_id=1, source_target_pairs={{0,6},{1,7},{2,4},{3,5},{4,2},{5,3},{6,0},{7,1},{8,14},{9,15},{10,... | collective-permute-start | bytes 6152 | tf_op jit(solution)/shard_map/ppermute | solution.py:206
  375.6 12.1 %collective-permute-start.36 = (bf16[2,1,2,1,256]{4,2,0,3,1:T(2,128)(2,1)S(1)}, bf16[2,1,2,1,256]{4,2,0,3,1:T(2,128)(2,1)S(1)}, u32[]{:S(2)}, u32[]{:S(2)}) collective-permute-start(bf16[2,1,2,1,256]{4,2,0,3,1:T(2,128)(2,1)S(1)} %bitcast.884), channel_id=1, source_target_pairs={{0,7},{1,6},{2,5},{3,4},{4,3},{5,2},{6,1},{7,0},{8,15},{9,14},{10,... | collective-permute-start | bytes 6152 | tf_op jit(solution)/shard_map/ppermute | solution.py:206
  378.8 9.6 %collective-permute-start.37 = (bf16[2,1,2,1,256]{4,2,0,3,1:T(2,128)(2,1)S(1)}, bf16[2,1,2,1,256]{4,2,0,3,1:T(2,128)(2,1)S(1)}, u32[]{:S(2)}, u32[]{:S(2)}) collective-permute-start(bf16[2,1,2,1,256]{4,2,0,3,1:T(2,128)(2,1)S(1)} %bitcast.871), channel_id=1, source_target_pairs={{0,8},{1,9},{2,10},{3,11},{4,12},{5,13},{6,14},{7,15},{8,0},{9,1},... | collective-permute-start | bytes 6152 | tf_op jit(solution)/shard_map/ppermute | solution.py:206
  379.4 12.2 %collective-permute-start.38 = (bf16[2,1,2,1,256]{4,2,0,3,1:T(2,128)(2,1)S(1)}, bf16[2,1,2,1,256]{4,2,0,3,1:T(2,128)(2,1)S(1)}, u32[]{:S(2)}, u32[]{:S(2)}) collective-permute-start(bf16[2,1,2,1,256]{4,2,0,3,1:T(2,128)(2,1)S(1)} %bitcast.864), channel_id=1, source_target_pairs={{0,9},{1,8},{2,11},{3,10},{4,13},{5,12},{6,15},{7,14},{8,1},{9,0},... | collective-permute-start | bytes 6152 | tf_op jit(solution)/shard_map/ppermute | solution.py:206
  381.9 10.4 %collective-permute-start.39 = (bf16[2,1,2,1,256]{4,2,0,3,1:T(2,128)(2,1)S(1)}, bf16[2,1,2,1,256]{4,2,0,3,1:T(2,128)(2,1)S(1)}, u32[]{:S(2)}, u32[]{:S(2)}) collective-permute-start(bf16[2,1,2,1,256]{4,2,0,3,1:T(2,128)(2,1)S(1)} %bitcast.856), channel_id=1, source_target_pairs={{0,10},{1,11},{2,8},{3,9},{4,14},{5,15},{6,12},{7,13},{8,2},{9,3},... | collective-permute-start | bytes 6152 | tf_op jit(solution)/shard_map/ppermute | solution.py:206
  383.6 13.8 %collective-permute-start.40 = (bf16[2,1,2,1,256]{4,2,0,3,1:T(2,128)(2,1)S(1)}, bf16[2,1,2,1,256]{4,2,0,3,1:T(2,128)(2,1)S(1)}, u32[]{:S(2)}, u32[]{:S(2)}) collective-permute-start(bf16[2,1,2,1,256]{4,2,0,3,1:T(2,128)(2,1)S(1)} %bitcast.872), channel_id=1, source_target_pairs={{0,11},{1,10},{2,9},{3,8},{4,15},{5,14},{6,13},{7,12},{8,3},{9,2},... | collective-permute-start | bytes 6152 | tf_op jit(solution)/shard_map/ppermute | solution.py:206
  387.7 9.7 %collective-permute-start.41 = (bf16[2,1,2,1,256]{4,2,0,3,1:T(2,128)(2,1)S(1)}, bf16[2,1,2,1,256]{4,2,0,3,1:T(2,128)(2,1)S(1)}, u32[]{:S(2)}, u32[]{:S(2)}) collective-permute-start(bf16[2,1,2,1,256]{4,2,0,3,1:T(2,128)(2,1)S(1)} %bitcast.865), channel_id=1, source_target_pairs={{0,12},{1,13},{2,14},{3,15},{4,8},{5,9},{6,10},{7,11},{8,4},{9,5},... | collective-permute-start | bytes 6152 | tf_op jit(solution)/shard_map/ppermute | solution.py:206
  388.4 9.0 %collective-permute-start.42 = (bf16[2,1,2,1,256]{4,2,0,3,1:T(2,128)(2,1)S(1)}, bf16[2,1,2,1,256]{4,2,0,3,1:T(2,128)(2,1)S(1)}, u32[]{:S(2)}, u32[]{:S(2)}) collective-permute-start(bf16[2,1,2,1,256]{4,2,0,3,1:T(2,128)(2,1)S(1)} %bitcast.859), channel_id=1, source_target_pairs={{0,13},{1,12},{2,15},{3,14},{4,9},{5,8},{6,11},{7,10},{8,5},{9,4},... | collective-permute-start | bytes 6152 | tf_op jit(solution)/shard_map/ppermute | solution.py:206
  392.3 7.2 %collective-permute-start.44 = (bf16[2,1,2,1,256]{4,2,0,3,1:T(2,128)(2,1)S(1)}, bf16[2,1,2,1,256]{4,2,0,3,1:T(2,128)(2,1)S(1)}, u32[]{:S(2)}, u32[]{:S(2)}) collective-permute-start(bf16[2,1,2,1,256]{4,2,0,3,1:T(2,128)(2,1)S(1)} %bitcast.847), channel_id=1, source_target_pairs={{0,15},{1,14},{2,13},{3,12},{4,11},{5,10},{6,9},{7,8},{8,7},{9,6},... | collective-permute-start | bytes 6152 | tf_op jit(solution)/shard_map/ppermute | solution.py:206
  (167 other events, 860.4 us)
Sparse Core Ops, SparseCore 0:
  411.1 133.2 all-reduce.3
